TPU v7x, 32 devices: a whole 2x2x4 slice. The times are simulated.
32 devices in a mesh: dp: 8 (over y, x, core), mp: 4 (over z).
Axes of the slice: x: 2, y: 2, z: 4, core: 2. Of those that a mesh axis runs over, the one named last changes fastest.
Arguments:
- inputs: bfloat16 [8192, 2048], P('dp'), may hold values from -8 to 8
- segment_ids: int32 [8, 1024], P('dp'), may hold values from 0 to 4, as said below
- pad_count: int32 [8], P('dp'), may hold values from 0 to 128, as said below
- layer_norm_gain: float32 [2048], replicated, may hold values from 0.5 to 1.5
- layer_norm_bias: float32 [2048], replicated, may hold values from -1.75 to 1.75
- qkv_weight: bfloat16 [2048, 3, 2048], P(None, None, 'mp'), may hold values from -0.125 to 0.125
- qkv_bias: float32 [3, 2048], P(None, 'mp'), may hold values from -1.75 to 1.75
- out_weight: bfloat16 [2048, 2048], P('mp'), may hold values from -1 to 1
- gateup_weight: bfloat16 [2048, 2, 5632], P(None, None, 'mp'), may hold values from -0.125 to 0.125
- down_weight: bfloat16 [5632, 2048], P('mp'), may hold values from -0.078125 to 0.078125
- y_grad: bfloat16 [8192, 2048], P('dp'), may hold values from -8 to 8
Outputs:
- output: bfloat16 [8192, 2048], P('dp')
- x_grad: bfloat16 [8192, 2048], P('dp')
- ln_gain_grad: float32 [2048], replicated
- ln_bias_grad: float32 [2048], replicated
- qkv_weight_grad: float32 [2048, 3, 2048], P('dp', None, 'mp')
- qkv_bias_grad: float32 [3, 2048], P(None, 'mp')
- out_weight_grad: float32 [2048, 2048], P('mp', 'dp')
- gateup_weight_grad: float32 [2048, 2, 5632], P('dp', None, 'mp')
- down_weight_grad: float32 [5632, 2048], P('mp', 'dp')
Inputs may be any that keep to these rules, and one draw needn't show every extreme that they name: `segment_ids`: within a row the ids never fall and run from 0 to 4 - 1 over the row's documents, each of 1 or more tokens and one of exactly 512; the row's last pad_count slots carry id 4. `pad_count`: some row has 128 padded slots and some row has none.
All inputs are finite; a program needn't handle non-finite values.
Results may differ from a plain program's by a relative error of at most 0.012.
The roundings to bfloat16 on the way count: a program that leaves them out, or rounds other values in their place, can miss the bound.
Values may be sent and summed in bfloat16 or wider, within the bound.
No kernel may reach another device: no remote copies, remote signals or barrier semaphores. Data moves between devices by JAX's collectives and lax.ppermute only.
A program may use at most 256 MiB of HBM per device.

v0:
```python
import jax
import jax.numpy as jnp
from jax import lax
from jax.sharding import PartitionSpec as P

HEAD_DIM = 64
ROT = 16
DOCS = 4
EPS = 1e-05


def tables(seg, padding, count):
    steps = jnp.arange(count, dtype=jnp.int32)
    onehot = (seg[:, None] == jnp.arange(DOCS + 1, dtype=jnp.int32)[None, :]).astype(jnp.int32)
    counts = jnp.sum(onehot, axis=0)
    before = jnp.cumsum(counts) - counts
    start = jnp.sum(onehot * before[None, :], axis=1)
    half = ROT // 2
    freq = jnp.power(10000.0, -2.0 * jnp.arange(half, dtype=jnp.float32) / ROT)
    angle = (steps - start).astype(jnp.float32)[:, None] * freq[None, :]
    return (jnp.cos(angle)[:, None, :], jnp.sin(angle)[:, None, :], steps < count - padding)


def rotate(value, cosine, sine):
    half = ROT // 2
    first = value[..., :half]
    second = value[..., half:ROT]
    return jnp.concatenate(
        [first * cosine - second * sine, second * cosine + first * sine, value[..., ROT:]], axis=-1
    )


def unrotate(value, cosine, sine):
    half = ROT // 2
    first = value[..., :half]
    second = value[..., half:ROT]
    return jnp.concatenate(
        [first * cosine + second * sine, second * cosine - first * sine, value[..., ROT:]], axis=-1
    )


def allowed_mask(start, block_rows, seg, valid):
    count = seg.shape[0]
    rows = start + jnp.arange(block_rows, dtype=jnp.int32)
    cols = jnp.arange(count, dtype=jnp.int32)
    seg_rows = lax.dynamic_slice_in_dim(seg, start, block_rows, 0)
    allowed = (
        (seg_rows[:, None] == seg[None, :]) & (cols[None, :] <= rows[:, None]) & valid[None, :]
    )
    return allowed | (cols[None, :] == rows[:, None])


def scores(start, block_rows, query, key, seg, valid):
    part = lax.dynamic_slice_in_dim(query, start, block_rows, 0)
    score = jnp.einsum(
        "qhd,khd->hqk", part, key, preferred_element_type=jnp.float32
    ) * HEAD_DIM ** (-0.5)
    allowed = allowed_mask(start, block_rows, seg, valid)
    return (part, jnp.where(allowed[None], score, -1e30), allowed)


def shards(
    inputs,
    segment_ids,
    pad_count,
    layer_norm_gain,
    layer_norm_bias,
    qkv_weight,
    qkv_bias,
    out_weight,
    gateup_weight,
    down_weight,
    y_grad,
):
    count, width = inputs.shape
    local = qkv_weight.shape[2]
    hidden_here = gateup_weight.shape[2]
    heads_here = local // HEAD_DIM
    seg = segment_ids[0]
    cosine, sine, valid = tables(seg, pad_count[0], count)
    valid_f = valid.astype(jnp.float32)
    xf = inputs.astype(jnp.float32)
    row_average = jnp.mean(xf, axis=-1, keepdims=True)
    mean_removed = xf - row_average
    var = jnp.mean(mean_removed * mean_removed, axis=-1, keepdims=True)
    inverse_deviation = lax.rsqrt(var + EPS)
    standardized_input = mean_removed * inverse_deviation
    norm_output = (standardized_input * layer_norm_gain + layer_norm_bias).astype(jnp.bfloat16)
    qkv = jnp.dot(
        norm_output, qkv_weight.reshape(width, 3 * local), preferred_element_type=jnp.float32
    )
    qkv = qkv.reshape(count, 3, local) + qkv_bias
    query = rotate(qkv[:, 0].reshape(count, heads_here, HEAD_DIM), cosine, sine).astype(
        jnp.bfloat16
    )
    key = rotate(qkv[:, 1].reshape(count, heads_here, HEAD_DIM), cosine, sine).astype(jnp.bfloat16)
    value = qkv[:, 2].reshape(count, heads_here, HEAD_DIM).astype(jnp.bfloat16)
    block_rows = min(512, count)
    starts = jnp.arange(count // block_rows, dtype=jnp.int32) * block_rows

    def forward_block(start):
        part, score, allowed = scores(start, block_rows, query, key, seg, valid)
        top = jnp.max(score, axis=-1, keepdims=True)
        expo = jnp.exp(score - top)
        total = jnp.sum(expo, axis=-1, keepdims=True)
        prob = (expo / total).astype(jnp.bfloat16)
        return (
            jnp.einsum("hqk,khd->qhd", prob, value, preferred_element_type=jnp.float32),
            (top + jnp.log(total))[..., 0],
        )

    attn_blocks, log_sums = lax.map(forward_block, starts)
    attn = (attn_blocks.reshape(count, local) * valid_f[:, None]).astype(jnp.bfloat16)
    gateup = jnp.dot(
        norm_output,
        gateup_weight.reshape(width, 2 * hidden_here),
        preferred_element_type=jnp.float32,
    )
    gateup = gateup.reshape(count, 2, hidden_here)
    gate = gateup[:, 0]
    upper = gateup[:, 1]
    sigma = jax.nn.sigmoid(gate)
    active = gate * sigma
    hidden = (active * upper).astype(jnp.bfloat16)
    partial_value = jnp.dot(attn, out_weight, preferred_element_type=jnp.float32) + jnp.dot(
        hidden, down_weight, preferred_element_type=jnp.float32
    )
    summed = lax.psum(partial_value, "mp")
    result = (xf + summed).astype(jnp.bfloat16)
    grad_out = jnp.einsum("ti,to->io", attn, y_grad, preferred_element_type=jnp.float32)
    grad_down = jnp.einsum("tf,to->fo", hidden, y_grad, preferred_element_type=jnp.float32)
    d_attn = jnp.einsum("to,io->ti", y_grad, out_weight, preferred_element_type=jnp.float32)
    d_attn = (d_attn.astype(jnp.bfloat16) * valid.astype(jnp.bfloat16)[:, None]).reshape(
        count, heads_here, HEAD_DIM
    )
    d_hidden = jnp.einsum("to,fo->tf", y_grad, down_weight, preferred_element_type=jnp.float32)
    d_gate = (d_hidden * upper * sigma * (1.0 + gate * (1.0 - sigma))).astype(jnp.bfloat16)
    d_upper = (d_hidden * active).astype(jnp.bfloat16)
    d_gateup = jnp.stack([d_gate, d_upper], axis=1)
    grad_gateup = jnp.einsum(
        "td,tjf->djf", norm_output, d_gateup, preferred_element_type=jnp.float32
    )

    def backward_block(carry, item):
        key_acc, value_acc = carry
        start, log_sum = item
        part, score, allowed = scores(start, block_rows, query, key, seg, valid)
        prob = jnp.where(allowed[None], jnp.exp(score - log_sum[..., None]), 0.0)
        prob_low = prob.astype(jnp.bfloat16)
        d_rows = lax.dynamic_slice_in_dim(d_attn, start, block_rows, 0)
        d_prob = jnp.einsum("qhd,khd->hqk", d_rows, value, preferred_element_type=jnp.float32)
        d_score = prob * (d_prob - jnp.sum(prob * d_prob, axis=-1, keepdims=True))
        d_score = d_score.astype(jnp.bfloat16)
        d_query = jnp.einsum(
            "hqk,khd->qhd", d_score, key, preferred_element_type=jnp.float32
        ) * HEAD_DIM ** (-0.5)
        key_acc = key_acc + jnp.einsum(
            "hqk,qhd->khd", d_score, part, preferred_element_type=jnp.float32
        ) * HEAD_DIM ** (-0.5)
        value_acc = value_acc + jnp.einsum(
            "hqk,qhd->khd", prob_low, d_rows, preferred_element_type=jnp.float32
        )
        return ((key_acc, value_acc), d_query)

    empty = jnp.zeros((count, heads_here, HEAD_DIM), jnp.float32)
    (d_key, d_value), d_queries = lax.scan(backward_block, (empty, empty), (starts, log_sums))
    d_query = unrotate(d_queries.reshape(count, heads_here, HEAD_DIM), cosine, sine)
    d_key = unrotate(d_key, cosine, sine)
    d_qkv = (
        jnp.stack([d_query, d_key, d_value], axis=1).reshape(count, 3, local).astype(jnp.bfloat16)
    )
    grad_qkv = jnp.einsum("td,tjc->djc", norm_output, d_qkv, preferred_element_type=jnp.float32)
    grad_bias = jnp.sum(d_qkv.astype(jnp.float32), axis=0)
    weight_sums = (
        lax.psum_scatter(grad_qkv, "dp", scatter_dimension=0, tiled=True),
        lax.psum_scatter(grad_out, "dp", scatter_dimension=1, tiled=True),
        lax.psum_scatter(grad_gateup, "dp", scatter_dimension=0, tiled=True),
        lax.psum_scatter(grad_down, "dp", scatter_dimension=1, tiled=True),
    )
    d_partial = jnp.einsum(
        "tjc,djc->td", d_qkv, qkv_weight, preferred_element_type=jnp.float32
    ) + jnp.einsum("tjf,djf->td", d_gateup, gateup_weight, preferred_element_type=jnp.float32)
    normalized_gradient = lax.psum(d_partial, "mp")
    gain_product = jnp.sum(normalized_gradient * standardized_input, axis=0)
    shift_part = jnp.sum(normalized_gradient, axis=0)
    gain_scaled = normalized_gradient * layer_norm_gain
    inner = (
        gain_scaled
        - jnp.mean(gain_scaled, axis=-1, keepdims=True)
        - standardized_input * jnp.mean(gain_scaled * standardized_input, axis=-1, keepdims=True)
    )
    input_grad = (y_grad.astype(jnp.float32) + inverse_deviation * inner).astype(jnp.bfloat16)
    bias_sum, gain_sum, shift_sum = lax.psum((grad_bias, gain_product, shift_part), "dp")
    return (
        result,
        input_grad,
        gain_sum,
        shift_sum,
        weight_sums[0],
        bias_sum,
        weight_sums[1],
        weight_sums[2],
        weight_sums[3],
    )


def solution(mesh):
    placed = (
        P("dp", None),
        P("dp", None),
        P("dp"),
        P(),
        P(),
        P(None, None, "mp"),
        P(None, "mp"),
        P("mp", None),
        P(None, None, "mp"),
        P("mp", None),
        P("dp", None),
    )
    return jax.shard_map(
        shards,
        mesh=mesh,
        in_specs=placed,
        out_specs=(
            P("dp", None),
            P("dp", None),
            P(),
            P(),
            P("dp", None, "mp"),
            P(None, "mp"),
            P("mp", "dp"),
            P("dp", None, "mp"),
            P("mp", "dp"),
        ),
        check_vma=False,
    )
```

profile of v0, /device:TPU:0, one launch (start us, length us, event | category | flops | bytes accessed | tf_op | source)
XLA Modules:
  0.0 1045.4 jit_solution(3423792791581384292)
XLA Ops:
  12.9 8.9 copy.39
  21.8 10.5 %broadcast_add_fusion = f32[1024,3,512]{0,2,1:T(8,128)S(1)} fusion(f32[3,512]{1,0:T(4,128)S(1)} %copy-done.24, bf16[2048,3,512]{0,2,1:T(8,128)(2,1)} %copy.39, bf16[1024,2048]{1,0:T(8,128)(2,1)} %param.15, f32[2048]{0:T(1024)S(1)} %copy-done.25, f32[2048]{0:T(1024)S(1)} %copy-done.21, f32[1024]{0:T(1024)S(1)} %add_rsqrt_fusion, ...), kind=kOutput, calls=%fused_computation.86 | convolution fusion | flops 6456606720 | bytes 16807936 | tf_op jit(solution)/shard_map/dot_general | solution.py:89
  45.3 79.3 %while.28 = (s32[]{:T(128)}, f32[2,512,8,64]{1,0,3,2:T(2,128)}, f32[2,8,512]{2,1,0:T(8,128)S(1)}, s32[2]{0:T(128)S(1)}, s32[1024]{0:T(1024)S(1)}, /*index=5*/s32...) while((s32[]{:T(128)}, f32[2,512,8,64]{1,0,3,2:T(2,128)}, ...), condition=%wide.region_8.9_spmd.clone, body=%wide.region_5.8_spmd.clone.sunk | while | flops 1127216640 | bytes 64635104 | solution.py:112
  65.5 19.6 %dynamic_update_slice.19 = f32[2,512,8,64]{1,0,3,2:T(2,128)} dynamic-update-slice(f32[2,512,8,64]{1,0,3,2:T(2,128)} %get-tuple-element.475, f32[1,512,8,64]{1,0,3,2:T(1,128)} %copy.73, s32[]{:T(128)} %get-tuple-element.474, s32[]{:T(128)} %constant.40.clone.1..sunk, s32[]{:T(128)} %constant.40.clone.1..sunk, s32[]{:T(128)} %constant.40.clone.1..sunk) | dynamic-update-slice | bytes 2097156 | tf_op jit(solution)/shard_map/while/body/jit(dynamic_update_index_in_dim)/dynamic_update_slice | solution.py:112
  104.9 19.6 %dynamic_update_slice.19 = f32[2,512,8,64]{1,0,3,2:T(2,128)} dynamic-update-slice(f32[2,512,8,64]{1,0,3,2:T(2,128)} %get-tuple-element.475, f32[1,512,8,64]{1,0,3,2:T(1,128)} %copy.73, s32[]{:T(128)} %get-tuple-element.474, s32[]{:T(128)} %constant.40.clone.1..sunk, s32[]{:T(128)} %constant.40.clone.1..sunk, s32[]{:T(128)} %constant.40.clone.1..sunk) | dynamic-update-slice | bytes 2097156 | tf_op jit(solution)/shard_map/while/body/jit(dynamic_update_index_in_dim)/dynamic_update_slice | solution.py:112
  132.1 159.0 %while.29 = (s32[]{:T(128)}, f32[1024,8,64]{0,2,1:T(8,128)}, f32[1024,8,64]{0,2,1:T(8,128)}, f32[2,512,8,64]{1,0,3,2:T(2,128)}, s32[2]{0:T(128)S(1)}, /*index=5*...) while((s32[]{:T(128)}, f32[1024,8,64]{0,2,1:T(8,128)}, ...), condition=%wide.region_12.13_spmd.clone, body=%wide.region_10.12_spmd.clone.sunk | while | flops 2732324352 | bytes 187793712 | solution.py:166
  136.4 9.7 fusion.130
  146.1 13.8 %multiply_reduce_fusion.3 = (f32[8,512]{1,0:T(8,128)S(1)}, f32[8,512,1024]{2,1,0:T(8,128)}) fusion(f32[8,512,1024]{2,1,0:T(8,128)} %fusion.130, f32[8,512]{1,0:T(8,128)S(1)} %dynamic-slice_bitcast_fusion.2, bf16[1024,8,64]{0,2,1:T(8,128)(2,1)S(1)} %get-tuple-element.540, bf16[1024,8,64]{0,2,1:T(8,128)(2,1)S(1)} %copy-done.4, s32[]{:T(128)S(6)} %select_n.47, ...), kind=kOutput, calls=%fused_computation.23.clone.1 | convolution fusion | flops 562032640 | bytes 35684356 | tf_op jit(solution)/shard_map/while/body/eval_jaxpr/qhd,khd->hqk/dot_general | solution.py:55
  159.9 11.3 %multiply_convert_fusion.8 = bf16[8,512,1024]{2,1,0:T(8,128)(2,1)S(1)} fusion(f32[8,512,1024]{2,1,0:T(8,128)} %get-tuple-element.459, f32[8,512,1024]{2,1,0:T(8,128)} %fusion.130, f32[8,512]{1,0:T(8,128)S(1)} %get-tuple-element.460), kind=kLoop, calls=%fused_computation.22.clone.1 | loop fusion | flops 12582912 | bytes 41959424 | tf_op jit(solution)/shard_map/while/body/eval_jaxpr/convert_element_type | solution.py:153
  176.0 19.6 %dynamic_update_slice.20 = f32[2,512,8,64]{1,0,3,2:T(2,128)} dynamic-update-slice(f32[2,512,8,64]{1,0,3,2:T(2,128)} %get-tuple-element.519, f32[1,512,8,64]{1,0,3,2:T(1,128)} %copy.74, s32[]{:T(128)} %get-tuple-element.516, s32[]{:T(128)} %constant.40.clone.1..sunk.1, s32[]{:T(128)} %constant.40.clone.1..sunk.1, s32[]{:T(128)} %constant.40.clone.1..sunk.1) | dynamic-update-slice | bytes 2097156 | tf_op jit(solution)/shard_map/while/body/jit(dynamic_update_index_in_dim)/dynamic_update_slice | solution.py:112
  202.3 8.7 bitcast_add_fusion.6
  215.2 9.7 fusion.130
  224.8 13.7 %multiply_reduce_fusion.3 = (f32[8,512]{1,0:T(8,128)S(1)}, f32[8,512,1024]{2,1,0:T(8,128)}) fusion(f32[8,512,1024]{2,1,0:T(8,128)} %fusion.130, f32[8,512]{1,0:T(8,128)S(1)} %dynamic-slice_bitcast_fusion.2, bf16[1024,8,64]{0,2,1:T(8,128)(2,1)S(1)} %get-tuple-element.540, bf16[1024,8,64]{0,2,1:T(8,128)(2,1)S(1)} %copy-done.4, s32[]{:T(128)S(6)} %select_n.47, ...), kind=kOutput, calls=%fused_computation.23.clone.1 | convolution fusion | flops 562032640 | bytes 35684356 | tf_op jit(solution)/shard_map/while/body/eval_jaxpr/qhd,khd->hqk/dot_general | solution.py:55
  238.6 11.3 %multiply_convert_fusion.8 = bf16[8,512,1024]{2,1,0:T(8,128)(2,1)S(1)} fusion(f32[8,512,1024]{2,1,0:T(8,128)} %get-tuple-element.459, f32[8,512,1024]{2,1,0:T(8,128)} %fusion.130, f32[8,512]{1,0:T(8,128)S(1)} %get-tuple-element.460), kind=kLoop, calls=%fused_computation.22.clone.1 | loop fusion | flops 12582912 | bytes 41959424 | tf_op jit(solution)/shard_map/while/body/eval_jaxpr/convert_element_type | solution.py:153
  254.7 19.6 %dynamic_update_slice.20 = f32[2,512,8,64]{1,0,3,2:T(2,128)} dynamic-update-slice(f32[2,512,8,64]{1,0,3,2:T(2,128)} %get-tuple-element.519, f32[1,512,8,64]{1,0,3,2:T(1,128)} %copy.74, s32[]{:T(128)} %get-tuple-element.516, s32[]{:T(128)} %constant.40.clone.1..sunk.1, s32[]{:T(128)} %constant.40.clone.1..sunk.1, s32[]{:T(128)} %constant.40.clone.1..sunk.1) | dynamic-update-slice | bytes 2097156 | tf_op jit(solution)/shard_map/while/body/jit(dynamic_update_index_in_dim)/dynamic_update_slice | solution.py:112
  274.3 7.2 bitcast_add_fusion.5
  281.5 9.3 bitcast_add_fusion.6
  307.5 11.2 %copy.66 = bf16[256,8,2,1408]{3,1,2,0:T(8,128)(2,1)} copy(bf16[256,8,2,1408]{3,2,1,0:T(2,128)(2,1)} %bitcast.147) | data formatting | bytes 23068672
  318.8 15.2 %copy.41 = bf16[2816,2048]{1,0:T(8,128)(2,1)} copy(bf16[2816,2048]{0,1:T(8,128)(2,1)} %bitcast.143) | data formatting | bytes 23068672 | tf_op jit(solution)/shard_map/dot_general | solution.py:114
  334.0 19.1 %fusion.72 = f32[1024,2,1408]{2,0,1:T(8,128)} fusion(bf16[2,1408,2048]{2,1,0:T(8,128)(2,1)} %bitcast.148, bf16[1024,2048]{1,0:T(8,128)(2,1)} %param.15, f32[2048]{0:T(1024)S(1)} %copy-done.26, f32[2048]{0:T(1024)S(1)} %copy-done.22, f32[1024]{0:T(1024)S(1)} %copy-done.20, f32[1024]{0:T(1024)S(1)} %copy-done.18), kind=kOutput, calls=%fused_computation.130 | convolution fusion | flops 11823742976 | bytes 27287552 | tf_op jit(solution)/shard_map/dot_general | solution.py:114
  353.6 17.5 %fusion.59 = (bf16[1024,1,1408]{2,0,1:T(8,128)(2,1)}, bf16[1024,1,1408]{2,0,1:T(8,128)(2,1)}, bf16[1024,1408]{1,0:T(8,128)(2,1)}) fusion(f32[1024,2,1408]{2,0,1:T(8,128)} %fusion.72, bf16[1024,2048]{1,0:T(8,128)(2,1)} %param.25, bf16[1408,2048]{1,0:T(8,128)(2,1)} %param.24), kind=kOutput, calls=%fused_computation.88 | convolution fusion | flops 5927206912 | bytes 30146560 | tf_op jit(solution)/shard_map/to,fo->tf/dot_general | solution.py:136
  371.1 12.3 %fusion.76 = f32[1024,2048]{1,0:T(8,128)} fusion(bf16[1024,1408]{1,0:T(8,128)(2,1)} %get-tuple-element.292, bf16[1408,2048]{1,0:T(8,128)(2,1)} %param.24), kind=kOutput, calls=%fused_computation.132 | convolution fusion | flops 5905580032 | bytes 17039360 | tf_op jit(solution)/shard_map/dot_general | solution.py:125
  383.5 8.9 fusion.69
  392.4 20.2 %bitcast_add_fusion.2 = f32[1024,2048]{1,0:T(8,128)} fusion(f32[1024,2048,1]{1,0,2:T(8,128)} %fusion.69, bf16[2048,2,1408]{2,1,0:T(2,128)(2,1)} %param.23, bf16[1024,1,1408]{2,0,1:T(8,128)(2,1)} %get-tuple-element.291, bf16[1024,1,1408]{2,0,1:T(8,128)(2,1)} %get-tuple-element.290), kind=kOutput, calls=%fused_computation.69 | convolution fusion | flops 11816140800 | bytes 34078720 | tf_op jit(solution)/shard_map/tjf,djf->td/dot_general | solution.py:182
  412.7 9.1 convolution_add_fusion
  421.8 20.7 %fusion.57 = f32[2048,2,1408]{2,0,1:T(8,128)} fusion(bf16[1024,1,1408]{2,0,1:T(8,128)(2,1)} %get-tuple-element.291, bf16[1024,1,1408]{2,0,1:T(8,128)(2,1)} %get-tuple-element.290, bf16[1024,2048]{1,0:T(8,128)(2,1)} %param.15, f32[2048]{0:T(1024)S(1)} %copy-done.26, f32[2048]{0:T(1024)S(1)} %copy-done.22, f32[1024]{0:T(1024)S(1)} %copy-done.20, ...), kind=kOutput, calls=%fused_computation.84 | convolution fusion | flops 11835277312 | bytes 33054720 | tf_op jit(solution)/shard_map/td,tjf->djf/dot_general | solution.py:140
  442.6 7.1 fusion.63
  449.8 13.8 %fusion.77 = f32[1408,2048]{1,0:T(8,128)} fusion(bf16[1024,1408]{1,0:T(8,128)(2,1)} %get-tuple-element.292, bf16[1024,2048]{1,0:T(8,128)(2,1)} %param.25), kind=kOutput, calls=%fused_computation.133 | convolution fusion | flops 5905580032 | bytes 18612224 | tf_op jit(solution)/shard_map/tf,to->fo/dot_general | solution.py:131
  465.0 15.0 %fusion.68 = f32[2048,3,512]{2,0,1:T(8,128)} fusion(bf16[1024,1,512]{2,0,1:T(8,128)(2,1)} %copy.45, bf16[1024,1,512]{2,0,1:T(8,128)(2,1)} %copy.44, bf16[1024,1,512]{2,0,1:T(8,128)(2,1)S(1)} %copy-done.9, bf16[1024,2048]{1,0:T(8,128)(2,1)} %param.15, f32[2048]{0:T(1024)S(1)} %copy-done.26, f32[2048]{0:T(1024)S(1)} %copy-done.22, f32[1024]{0:T(1024)S(1)} %copy-done.20, ...), kind=kOutput, calls=%fused_computation.128 | convolution fusion | flops 6464471040 | bytes 19947520 | tf_op jit(solution)/shard_map/td,tjc->djc/dot_general | solution.py:172
  482.1 504.8 %all-reduce.4.cloned.1.call-done = (f32[1024,2048]{1,0:T(8,128)}, f32[1024,2048]{1,0:T(8,128)}) async-done(((f32[1024,2048]{1,0:T(8,128)}, f32[1024,2048]{1,0:T(8,128)}), (f32[1024,2048]{1,0:T(8,128)}, f32[1024,2048]{1,0:T(8,128)})) %all-reduce.4.cloned.1.call-update) | async-done | bytes 16777232 | tf_op jit(solution)/shard_map/psum | solution.py:128
  993.4 24.8 %all-reduce = (f32[2048]{0:T(1024)}, f32[2048]{0:T(1024)}, f32[3,512]{1,0:T(4,128)}) all-reduce(f32[2048]{0:T(1024)S(1)} %get-tuple-element.231, f32[2048]{0:T(1024)S(1)} %get-tuple-element.234, f32[3,512]{1,0:T(4,128)S(1)} %convert_reduce_fusion.1), channel_id=1, replica_groups=mesh['dp'=8,'mp'=4] {'dp'}, use_global_device_ids=true, to_apply=%region_17.18 | all-reduce | flops 5632 | bytes 45056 | tf_op jit(solution)/shard_map/psum | solution.py:193
  1018.2 13.6 %fusion.47 = (bf16[1024,2048]{1,0:T(8,128)(2,1)}, bf16[1024,2048]{1,0:T(8,128)(2,1)}) fusion(bf16[1024,2048]{1,0:T(8,128)(2,1)} %param.15, bf16[1024,2048]{1,0:T(8,128)(2,1)} %param.25, f32[1024,2048]{1,0:T(8,128)} %get-tuple-element.285, f32[1024]{0:T(1024)S(1)} %broadcast_multiply_fusion, f32[1024]{0:T(1024)S(1)} %broadcast_multiply_fusion.1, ...), kind=kLoop, calls=%fused_computation.65 | loop fusion | flops 27262976 | bytes 33579008 | tf_op jit(solution)/shard_map/convert_element_type | solution.py:192
  (160 shorter events, 113.3 us)
Async XLA Ops:
  8.0 116.5 %copy-start = (bf16[512,2048]{1,0:T(8,128)(2,1)S(1)}, bf16[512,2048]{1,0:T(8,128)(2,1)}, u32[]{:S(2)}) copy-start(bf16[512,2048]{1,0:T(8,128)(2,1)} %param.22) | copy-start | bytes 6291460
  8.0 978.9 %all-reduce.4.cloned.1.call-start = ((), (), s32[]{:S(2)}) async-start(), calls=%async_computation.8 | async-start | bytes 33554432 | tf_op jit(solution)/shard_map/psum | solution.py:128
  11.7 10.1 copy-start.17
  12.9 8.9 copy-start.19
  12.9 8.9 copy-start.21
  12.9 8.9 copy-start.24
  12.9 8.9 copy-start.25
  45.3 79.3 %copy-start.23 = (bf16[1024]{0:T(1024)(128)(2,1)S(1)}, bf16[1024]{0:T(1024)(128)(2,1)}, u32[]{:S(2)}) copy-start(bf16[1024]{0:T(1024)(128)(2,1)} %fusion.65) | copy-start | bytes 6148
  54.6 4.3 copy-start.2
  136.4 9.7 copy-start.4
  171.2 4.8 copy-start.1
  195.6 6.6 copy-start.5
  215.1 9.7 copy-start.4
  249.9 4.8 copy-start.1
  274.3 7.2 copy-start.5
  291.1 5.6 copy-start.14
  291.1 5.6 copy-start.16
  318.8 15.2 %copy-start.18 = (f32[1024]{0:T(1024)S(1)}, f32[1024]{0:T(1024)}, u32[]{:S(2)}) copy-start(f32[1024]{0:T(1024)} %copy-done.17) | copy-start | bytes 12292
  318.8 15.2 %copy-start.20 = (f32[1024]{0:T(1024)S(1)}, f32[1024]{0:T(1024)}, u32[]{:S(2)}) copy-start(f32[1024]{0:T(1024)} %copy-done.19) | copy-start | bytes 12292
  318.8 15.2 %copy-start.22 = (f32[2048]{0:T(1024)S(1)}, f32[2048]{0:T(1024)}, u32[]{:S(2)}) copy-start(f32[2048]{0:T(1024)} %param.18) | copy-start | bytes 24580
  318.8 15.2 %copy-start.26 = (f32[2048]{0:T(1024)S(1)}, f32[2048]{0:T(1024)}, u32[]{:S(2)}) copy-start(f32[2048]{0:T(1024)} %param.19) | copy-start | bytes 24580
  334.0 19.1 %copy-start.7 = (f32[2,512,8,64]{1,0,3,2:T(2,128)S(1)}, f32[2,512,8,64]{1,0,3,2:T(2,128)}, u32[]{:S(2)}) copy-start(f32[2,512,8,64]{1,0,3,2:T(2,128)} %get-tuple-element.131) | copy-start | bytes 6291460
  353.1 30.4 %slice-start = ((s8[6291456]{0:T(1024)(128)(4,1)}), s8[4194304]{0:T(1024)(128)(4,1)S(1)}, s32[]{:S(2)}) async-start(s8[6291456]{0:T(1024)(128)(4,1)} %bitcast.150), calls=%async_computation.9 | async-start | bytes 8388608
  353.5 59.2 %copy-start.6 = (f32[64,8,2,512]{3,1,2,0:T(8,128)}, f32[64,8,2,512]{3,1,2,0:T(8,128)S(1)}, u32[]{:S(2)}) copy-start(f32[64,8,2,512]{3,1,2,0:T(8,128)S(1)} %copy.65) | copy-start | bytes 6291460
  353.5 29.9 %slice-start.1 = ((s8[6291456]{0:T(1024)(128)(4,1)}), s8[2097152]{0:T(1024)(128)(4,1)S(1)}, s32[]{:S(2)}) async-start(s8[6291456]{0:T(1024)(128)(4,1)} %bitcast.150), calls=%async_computation.10 | async-start | bytes 4194304
  371.1 12.4 %copy-start.8 = (bf16[1024,1,512]{2,0,1:T(8,128)(2,1)S(1)}, bf16[1024,1,512]{2,0,1:T(8,128)(2,1)}, u32[]{:S(2)}) copy-start(bf16[1024,1,512]{2,0,1:T(8,128)(2,1)} %copy.43) | copy-start | bytes 3145732
  371.1 12.4 %copy-start.10 = (bf16[1024,1,512]{2,0,1:T(8,128)(2,1)S(1)}, bf16[1024,1,512]{2,0,1:T(8,128)(2,1)}, u32[]{:S(2)}) copy-start(bf16[1024,1,512]{2,0,1:T(8,128)(2,1)} %copy.44) | copy-start | bytes 3145732
  371.1 12.4 %copy-start.11 = (bf16[1024,1,512]{2,0,1:T(8,128)(2,1)S(1)}, bf16[1024,1,512]{2,0,1:T(8,128)(2,1)}, u32[]{:S(2)}) copy-start(bf16[1024,1,512]{2,0,1:T(8,128)(2,1)} %copy.45) | copy-start | bytes 3145732
  421.8 610.1 %reduce-scatter.9.cloned.1.call-start = ((), (), s32[]{:S(2)}) async-start(), calls=%async_computation.6 | async-start | bytes 25952256 | tf_op jit(solution)/shard_map/reduce_scatter | solution.py:177
  442.5 595.0 %reduce-scatter.7.cloned.1.call-start = ((), (), s32[]{:S(2)}) async-start(), calls=%async_computation.5 | async-start | bytes 4718592 | tf_op jit(solution)/shard_map/reduce_scatter | solution.py:176
  449.7 587.8 %reduce-scatter.11.cloned.1.call-start = ((), (), s32[]{:S(2)}) async-start(), calls=%async_computation.7 | async-start | bytes 12976128 | tf_op jit(solution)/shard_map/reduce_scatter | solution.py:178
  463.6 573.9 %reduce-scatter.5.cloned.1.call-start = ((), (), s32[]{:S(2)}) async-start(), calls=%async_computation.4 | async-start | bytes 14155776 | tf_op jit(solution)/shard_map/reduce_scatter | solution.py:175
  (6 other events, 15.6 us)
Sparse Core Ops, SparseCore 0:
  421.9 564.9 all-reduce.3
Sparse Core Ops, SparseCore 1:
  442.6 148.9 reduce-scatter.8
  595.3 50.9 reduce-scatter.6
  650.2 86.7 reduce-scatter.10
  741.0 91.8 reduce-scatter.4
where the time goes:
time: 1060 us; the launch traced here: 1050 us
  waiting for transfers between devices  505 us (48%)
  matrix products  262 us (25%)
  local copies, waits for them, and re-layouts  156 us (15%)
  other arithmetic  71.6 us (7%)
  blocking collectives  24.8 us (2%)
  between operations  17 us (2%)
    psum x1, waiting for transfers between devices, shards(): summed = lax.psum(partial_value, 'mp')  505 us
    dynamic_update_slice x8, local copies, waits for them, and re-layouts, shards(): attn_blocks, log_sums = lax.map(forward_block, starts)  86.9 us
    dot_general x4, matrix products, scores(): jnp.einsum('qhd,khd->hqk', part, key, preferred_element_type=jnp.float32)  36.8 us
    unnamed x54, local copies, waits for them, and re-layouts  28.3 us
    psum x1, blocking collectives, shards(): lax.psum((grad_bias, gain_product, shift_part), 'dp')  24.8 us
    convert_element_type x2, other arithmetic, backward_block(): d_score = d_score.astype(jnp.bfloat16)  22.7 us
  transfers between devices with their start and end apart: 5, of which 1 were waited for; matrix products, arithmetic and copies ran while one was open for 8% of the time, Pallas kernels for 0%

commit v1 on v0

--- a/solution.py
+++ b/solution.py
@@ -125,7 +125,9 @@
     partial_value = jnp.dot(attn, out_weight, preferred_element_type=jnp.float32) + jnp.dot(
         hidden, down_weight, preferred_element_type=jnp.float32
     )
-    summed = lax.psum(partial_value, "mp")
+    summed = partial_value
+    for hop in (1, 2):
+        summed = summed + lax.ppermute(summed, "mp", [(dev, dev ^ hop) for dev in range(4)])
     result = (xf + summed).astype(jnp.bfloat16)
     grad_out = jnp.einsum("ti,to->io", attn, y_grad, preferred_element_type=jnp.float32)
     grad_down = jnp.einsum("tf,to->fo", hidden, y_grad, preferred_element_type=jnp.float32)

time: 1060 us -> 1280 us (1.21)
  waiting for transfers between devices: 505 us -> 711 us
  other arithmetic: 71.6 us -> 87.6 us
    ppermute x0 -> x2, waiting for transfers between devices: none -> 711 us  [shards(): lax.ppermute(summed, 'mp', [(dev, dev ^ hop) for dev in range(4)])]
    psum x1, waiting for transfers between devices: 505 us -> 0.02 us  [shards(): normalized_gradient = lax.psum(d_partial, 'mp')]
  transfers between devices with their start and end apart: 5 -> 7, of which waited for: 1 -> 2; matrix products, arithmetic and copies ran while one was open for 8% -> 9% of each run, Pallas kernels for 0% -> 0%
where the time goes in v1:
time: 1280 us; the launch traced here: 1270 us
  waiting for transfers between devices  711 us (56%)
  matrix products  253 us (20%)
  local copies, waits for them, and re-layouts  162 us (13%)
  other arithmetic  87.6 us (7%)
  blocking collectives  24.6 us (2%)
  between operations  16.9 us (1%)
    ppermute x2, waiting for transfers between devices, shards(): lax.ppermute(summed, 'mp', [(dev, dev ^ hop) for dev in range(4)])  711 us
    dynamic_update_slice x8, local copies, waits for them, and re-layouts, shards(): attn_blocks, log_sums = lax.map(forward_block, starts)  86.9 us
    dot_general x4, matrix products, scores(): jnp.einsum('qhd,khd->hqk', part, key, preferred_element_type=jnp.float32)  36.8 us
    unnamed x54, local copies, waits for them, and re-layouts  33 us
  transfers between devices with their start and end apart: 7, of which 2 were waited for; matrix products, arithmetic and copies ran while one was open for 9% of the time, Pallas kernels for 0%

profile of v1, /device:TPU:0, one launch (start us, length us, event | category | flops | bytes accessed | tf_op | source)
XLA Modules:
  0.0 1269.4 jit_solution(2311608826617424284)
XLA Ops:
  12.9 8.9 copy.39
  21.8 10.5 broadcast_add_fusion
  45.3 78.9 %while.28 = (s32[]{:T(128)}, f32[2,512,8,64]{1,0,3,2:T(2,128)}, f32[2,8,512]{2,1,0:T(8,128)S(1)}, s32[2]{0:T(128)S(1)}, s32[1024]{0:T(1024)S(1)}, /*index=5*/s32...) while((s32[]{:T(128)}, f32[2,512,8,64]{1,0,3,2:T(2,128)}, ...), condition=%wide.region_8.9_spmd.clone, body=%wide.region_5.8_spmd.clone.sunk | while | flops 1127216640 | bytes 64635104 | solution.py:112
  65.2 19.6 %dynamic_update_slice.19 = f32[2,512,8,64]{1,0,3,2:T(2,128)} dynamic-update-slice(f32[2,512,8,64]{1,0,3,2:T(2,128)} %get-tuple-element.473, f32[1,512,8,64]{1,0,3,2:T(1,128)} %copy.73, s32[]{:T(128)} %get-tuple-element.472, s32[]{:T(128)} %constant.40.clone.1..sunk, s32[]{:T(128)} %constant.40.clone.1..sunk, s32[]{:T(128)} %constant.40.clone.1..sunk) | dynamic-update-slice | bytes 2097156 | tf_op jit(solution)/shard_map/while/body/jit(dynamic_update_index_in_dim)/dynamic_update_slice | solution.py:112
  104.6 19.6 %dynamic_update_slice.19 = f32[2,512,8,64]{1,0,3,2:T(2,128)} dynamic-update-slice(f32[2,512,8,64]{1,0,3,2:T(2,128)} %get-tuple-element.473, f32[1,512,8,64]{1,0,3,2:T(1,128)} %copy.73, s32[]{:T(128)} %get-tuple-element.472, s32[]{:T(128)} %constant.40.clone.1..sunk, s32[]{:T(128)} %constant.40.clone.1..sunk, s32[]{:T(128)} %constant.40.clone.1..sunk) | dynamic-update-slice | bytes 2097156 | tf_op jit(solution)/shard_map/while/body/jit(dynamic_update_index_in_dim)/dynamic_update_slice | solution.py:112
  131.7 159.2 %while.29 = (s32[]{:T(128)}, f32[1024,8,64]{0,2,1:T(8,128)}, f32[1024,8,64]{0,2,1:T(8,128)}, f32[2,512,8,64]{1,0,3,2:T(2,128)}, s32[2]{0:T(128)S(1)}, /*index=5*...) while((s32[]{:T(128)}, f32[1024,8,64]{0,2,1:T(8,128)}, ...), condition=%wide.region_11.12_spmd.clone, body=%wide.region_9.11_spmd.clone.sunk | while | flops 2732324352 | bytes 187793712 | solution.py:168
  136.1 9.7 fusion.130
  145.8 13.7 %multiply_reduce_fusion.3 = (f32[8,512]{1,0:T(8,128)S(1)}, f32[8,512,1024]{2,1,0:T(8,128)}) fusion(f32[8,512,1024]{2,1,0:T(8,128)} %fusion.130, f32[8,512]{1,0:T(8,128)S(1)} %dynamic-slice_bitcast_fusion.2, bf16[1024,8,64]{0,2,1:T(8,128)(2,1)S(1)} %get-tuple-element.538, bf16[1024,8,64]{0,2,1:T(8,128)(2,1)S(1)} %copy-done.5, s32[]{:T(128)S(6)} %select_n.47, ...), kind=kOutput, calls=%fused_computation.23.clone.1 | convolution fusion | flops 562032640 | bytes 35684356 | tf_op jit(solution)/shard_map/while/body/eval_jaxpr/qhd,khd->hqk/dot_general | solution.py:55
  159.5 11.3 multiply_convert_fusion.8
  175.7 19.6 %dynamic_update_slice.20 = f32[2,512,8,64]{1,0,3,2:T(2,128)} dynamic-update-slice(f32[2,512,8,64]{1,0,3,2:T(2,128)} %get-tuple-element.517, f32[1,512,8,64]{1,0,3,2:T(1,128)} %copy.74, s32[]{:T(128)} %get-tuple-element.514, s32[]{:T(128)} %constant.40.clone.1..sunk.1, s32[]{:T(128)} %constant.40.clone.1..sunk.1, s32[]{:T(128)} %constant.40.clone.1..sunk.1) | dynamic-update-slice | bytes 2097156 | tf_op jit(solution)/shard_map/while/body/jit(dynamic_update_index_in_dim)/dynamic_update_slice | solution.py:112
  202.0 8.7 bitcast_add_fusion.6
  214.8 9.7 fusion.130
  224.5 13.7 %multiply_reduce_fusion.3 = (f32[8,512]{1,0:T(8,128)S(1)}, f32[8,512,1024]{2,1,0:T(8,128)}) fusion(f32[8,512,1024]{2,1,0:T(8,128)} %fusion.130, f32[8,512]{1,0:T(8,128)S(1)} %dynamic-slice_bitcast_fusion.2, bf16[1024,8,64]{0,2,1:T(8,128)(2,1)S(1)} %get-tuple-element.538, bf16[1024,8,64]{0,2,1:T(8,128)(2,1)S(1)} %copy-done.5, s32[]{:T(128)S(6)} %select_n.47, ...), kind=kOutput, calls=%fused_computation.23.clone.1 | convolution fusion | flops 562032640 | bytes 35684356 | tf_op jit(solution)/shard_map/while/body/eval_jaxpr/qhd,khd->hqk/dot_general | solution.py:55
  238.2 11.3 multiply_convert_fusion.8
  254.4 19.6 %dynamic_update_slice.20 = f32[2,512,8,64]{1,0,3,2:T(2,128)} dynamic-update-slice(f32[2,512,8,64]{1,0,3,2:T(2,128)} %get-tuple-element.517, f32[1,512,8,64]{1,0,3,2:T(1,128)} %copy.74, s32[]{:T(128)} %get-tuple-element.514, s32[]{:T(128)} %constant.40.clone.1..sunk.1, s32[]{:T(128)} %constant.40.clone.1..sunk.1, s32[]{:T(128)} %constant.40.clone.1..sunk.1) | dynamic-update-slice | bytes 2097156 | tf_op jit(solution)/shard_map/while/body/jit(dynamic_update_index_in_dim)/dynamic_update_slice | solution.py:112
  274.0 7.2 bitcast_add_fusion.5
  281.2 9.3 bitcast_add_fusion.6
  312.4 11.2 copy.66
  323.6 15.2 %copy.41 = bf16[2816,2048]{1,0:T(8,128)(2,1)} copy(bf16[2816,2048]{0,1:T(8,128)(2,1)} %bitcast.143) | data formatting | bytes 23068672 | tf_op jit(solution)/shard_map/dot_general | solution.py:114
  338.8 19.1 %fusion.72 = f32[1024,2,1408]{2,0,1:T(8,128)} fusion(bf16[2,1408,2048]{2,1,0:T(8,128)(2,1)} %bitcast.148, bf16[1024,2048]{1,0:T(8,128)(2,1)} %param.15, f32[2048]{0:T(1024)S(1)} %copy-done.26, f32[2048]{0:T(1024)S(1)} %copy-done.22, f32[1024]{0:T(1024)S(1)} %copy-done.20, f32[1024]{0:T(1024)S(1)} %copy-done.18), kind=kOutput, calls=%fused_computation.130 | convolution fusion | flops 11823742976 | bytes 27287552 | tf_op jit(solution)/shard_map/dot_general | solution.py:114
  357.9 16.7 %fusion.59 = (bf16[1024,1,1408]{2,0,1:T(8,128)(2,1)}, bf16[1024,1,1408]{2,0,1:T(8,128)(2,1)}, bf16[1024,1408]{1,0:T(8,128)(2,1)}) fusion(f32[1024,2,1408]{2,0,1:T(8,128)} %fusion.72, bf16[1024,2048]{1,0:T(8,128)(2,1)} %param.25, bf16[1408,2048]{1,0:T(8,128)(2,1)} %param.24), kind=kOutput, calls=%fused_computation.88 | convolution fusion | flops 5927206912 | bytes 30146560 | tf_op jit(solution)/shard_map/to,fo->tf/dot_general | solution.py:138
  374.6 10.2 fusion.69
  384.8 20.2 %bitcast_add_fusion.2 = f32[1024,2048]{1,0:T(8,128)} fusion(f32[1024,2048,1]{1,0,2:T(8,128)} %fusion.69, bf16[2048,2,1408]{2,1,0:T(2,128)(2,1)} %param.23, bf16[1024,1,1408]{2,0,1:T(8,128)(2,1)} %get-tuple-element.289, bf16[1024,1,1408]{2,0,1:T(8,128)(2,1)} %get-tuple-element.288), kind=kOutput, calls=%fused_computation.69 | convolution fusion | flops 11816140800 | bytes 34078720 | tf_op jit(solution)/shard_map/tjf,djf->td/dot_general | solution.py:184
  405.0 20.9 %fusion.57 = f32[2048,2,1408]{2,0,1:T(8,128)} fusion(bf16[1024,1,1408]{2,0,1:T(8,128)(2,1)} %get-tuple-element.289, bf16[1024,1,1408]{2,0,1:T(8,128)(2,1)} %get-tuple-element.288, bf16[1024,2048]{1,0:T(8,128)(2,1)} %param.15, f32[2048]{0:T(1024)S(1)} %copy-done.26, f32[2048]{0:T(1024)S(1)} %copy-done.22, f32[1024]{0:T(1024)S(1)} %copy-done.20, ...), kind=kOutput, calls=%fused_computation.84 | convolution fusion | flops 11835277312 | bytes 33054720 | tf_op jit(solution)/shard_map/td,tjf->djf/dot_general | solution.py:142
  436.0 13.9 %fusion.77 = f32[1408,2048]{1,0:T(8,128)} fusion(bf16[1024,1408]{1,0:T(8,128)(2,1)} %get-tuple-element.290, bf16[1024,2048]{1,0:T(8,128)(2,1)} %param.25), kind=kOutput, calls=%fused_computation.133 | convolution fusion | flops 5905580032 | bytes 18612224 | tf_op jit(solution)/shard_map/tf,to->fo/dot_general | solution.py:133
  449.9 15.4 %fusion.68 = f32[2048,3,512]{2,0,1:T(8,128)} fusion(bf16[1024,1,512]{2,0,1:T(8,128)(2,1)} %copy.45, bf16[1024,1,512]{2,0,1:T(8,128)(2,1)} %copy.44, bf16[1024,1,512]{2,0,1:T(8,128)(2,1)S(1)} %copy.43, bf16[1024,2048]{1,0:T(8,128)(2,1)} %param.15, f32[2048]{0:T(1024)S(1)} %copy-done.26, f32[2048]{0:T(1024)S(1)} %copy-done.22, f32[1024]{0:T(1024)S(1)} %copy-done.20, ...), kind=kOutput, calls=%fused_computation.128 | convolution fusion | flops 6464471040 | bytes 19947520 | tf_op jit(solution)/shard_map/td,tjc->djc/dot_general | solution.py:174
  465.4 9.7 fusion.76
  484.5 380.3 %collective-permute-done = f32[1024,2048]{1,0:T(8,128)} collective-permute-done((f32[1024,2048]{1,0:T(8,128)S(1)}, f32[1024,2048]{1,0:T(8,128)}, u32[]{:S(2)}, u32[]{:S(2)}) %collective-permute-start) | collective-permute-done | bytes 8388640 | tf_op jit(solution)/shard_map/ppermute | solution.py:130
  864.7 11.8 add.145
  884.1 24.6 %all-reduce = (f32[2048]{0:T(1024)}, f32[2048]{0:T(1024)}, f32[3,512]{1,0:T(4,128)}) all-reduce(f32[2048]{0:T(1024)S(1)} %get-tuple-element.231, f32[2048]{0:T(1024)S(1)} %get-tuple-element.234, f32[3,512]{1,0:T(4,128)S(1)} %convert_reduce_fusion.1), channel_id=1, replica_groups=mesh['dp'=8,'mp'=4] {'dp'}, use_global_device_ids=true, to_apply=%region_16.17 | all-reduce | flops 5632 | bytes 45056 | tf_op jit(solution)/shard_map/psum | solution.py:195
  908.7 331.0 %collective-permute-done.1 = f32[1024,2048]{1,0:T(8,128)} collective-permute-done((f32[1024,2048]{1,0:T(8,128)}, f32[1024,2048]{1,0:T(8,128)}, u32[]{:S(2)}, u32[]{:S(2)}) %collective-permute-start.1) | collective-permute-done | bytes 8388640 | tf_op jit(solution)/shard_map/ppermute | solution.py:130
  1239.7 16.2 %fusion.47 = (bf16[1024,2048]{1,0:T(8,128)(2,1)}, bf16[1024,2048]{1,0:T(8,128)(2,1)}) fusion(bf16[1024,2048]{1,0:T(8,128)(2,1)} %param.15, bf16[1024,2048]{1,0:T(8,128)(2,1)} %param.25, f32[1024,2048]{1,0:T(8,128)} %all-reduce.3.cloned.1.call-done, f32[1024]{0:T(1024)S(1)} %broadcast_multiply_fusion, f32[1024]{0:T(1024)S(1)} %broadcast_multiply_fusion.1, ...), kind=kLoop, calls=%fused_computation.65 | loop fusion | flops 29360128 | bytes 41967616 | tf_op jit(solution)/shard_map/convert_element_type | solution.py:194
  (165 shorter events, 134.8 us)
Async XLA Ops:
  8.0 116.2 %copy-start = (bf16[512,2048]{1,0:T(8,128)(2,1)S(1)}, bf16[512,2048]{1,0:T(8,128)(2,1)}, u32[]{:S(2)}) copy-start(bf16[512,2048]{1,0:T(8,128)(2,1)} %param.22) | copy-start | bytes 6291460
  8.0 869.3 %all-reduce.3.cloned.1.call-start = ((), (), s32[]{:S(2)}) async-start(), calls=%async_computation.4 | async-start | bytes 16777216 | tf_op jit(solution)/shard_map/psum | solution.py:185
  11.7 10.1 copy-start.17
  12.9 8.9 copy-start.19
  12.9 8.9 copy-start.21
  12.9 8.9 copy-start.24
  12.9 8.9 copy-start.25
  45.3 78.9 %copy-start.23 = (bf16[1024]{0:T(1024)(128)(2,1)S(1)}, bf16[1024]{0:T(1024)(128)(2,1)}, u32[]{:S(2)}) copy-start(bf16[1024]{0:T(1024)(128)(2,1)} %fusion.65) | copy-start | bytes 6148
  136.1 9.7 copy-start.5
  170.9 4.8 copy-start.1
  195.3 6.6 copy-start.6
  214.8 9.7 copy-start.5
  249.6 4.8 copy-start.1
  274.0 7.2 copy-start.6
  290.9 5.6 copy-start.14
  290.9 5.6 copy-start.16
  323.6 15.2 %copy-start.18 = (f32[1024]{0:T(1024)S(1)}, f32[1024]{0:T(1024)}, u32[]{:S(2)}) copy-start(f32[1024]{0:T(1024)} %copy-done.17) | copy-start | bytes 12292
  323.6 15.2 %copy-start.20 = (f32[1024]{0:T(1024)S(1)}, f32[1024]{0:T(1024)}, u32[]{:S(2)}) copy-start(f32[1024]{0:T(1024)} %copy-done.19) | copy-start | bytes 12292
  323.6 15.2 %copy-start.22 = (f32[2048]{0:T(1024)S(1)}, f32[2048]{0:T(1024)}, u32[]{:S(2)}) copy-start(f32[2048]{0:T(1024)} %param.18) | copy-start | bytes 24580
  323.6 15.2 %copy-start.26 = (f32[2048]{0:T(1024)S(1)}, f32[2048]{0:T(1024)}, u32[]{:S(2)}) copy-start(f32[2048]{0:T(1024)} %param.19) | copy-start | bytes 24580
  338.8 35.8 %slice-start = ((s8[6291456]{0:T(1024)(128)(4,1)}), s8[4194304]{0:T(1024)(128)(4,1)S(1)}, s32[]{:S(2)}) async-start(s8[6291456]{0:T(1024)(128)(4,1)} %bitcast.150), calls=%async_computation.9 | async-start | bytes 8388608
  357.9 16.7 %slice-start.1 = ((s8[6291456]{0:T(1024)(128)(4,1)}), s8[2097152]{0:T(1024)(128)(4,1)S(1)}, s32[]{:S(2)}) async-start(s8[6291456]{0:T(1024)(128)(4,1)} %bitcast.150), calls=%async_computation.10 | async-start | bytes 4194304
  357.9 16.7 %copy-start.9 = (bf16[1024,1,512]{2,0,1:T(8,128)(2,1)S(1)}, bf16[1024,1,512]{2,0,1:T(8,128)(2,1)}, u32[]{:S(2)}) copy-start(bf16[1024,1,512]{2,0,1:T(8,128)(2,1)} %copy.44) | copy-start | bytes 3145732
  405.0 851.0 %reduce-scatter.9.cloned.1.call-start = ((), (), s32[]{:S(2)}) async-start(), calls=%async_computation.7 | async-start | bytes 25952256 | tf_op jit(solution)/shard_map/reduce_scatter | solution.py:179
  425.9 835.6 %reduce-scatter.7.cloned.1.call-start = ((), (), s32[]{:S(2)}) async-start(), calls=%async_computation.6 | async-start | bytes 4718592 | tf_op jit(solution)/shard_map/reduce_scatter | solution.py:178
  435.9 825.6 %reduce-scatter.11.cloned.1.call-start = ((), (), s32[]{:S(2)}) async-start(), calls=%async_computation.8 | async-start | bytes 12976128 | tf_op jit(solution)/shard_map/reduce_scatter | solution.py:180
  449.9 811.7 %reduce-scatter.5.cloned.1.call-start = ((), (), s32[]{:S(2)}) async-start(), calls=%async_computation.5 | async-start | bytes 14155776 | tf_op jit(solution)/shard_map/reduce_scatter | solution.py:177
  465.3 9.7 copy-start.8
  480.8 396.1 %copy-start.10 = (bf16[1024,1,512]{2,0,1:T(8,128)(2,1)S(1)}, bf16[1024,1,512]{2,0,1:T(8,128)(2,1)}, u32[]{:S(2)}) copy-start(bf16[1024,1,512]{2,0,1:T(8,128)(2,1)} %copy.44) | copy-start | bytes 3145732
  480.8 396.1 %copy-start.11 = (bf16[1024,1,512]{2,0,1:T(8,128)(2,1)S(1)}, bf16[1024,1,512]{2,0,1:T(8,128)(2,1)}, u32[]{:S(2)}) copy-start(bf16[1024,1,512]{2,0,1:T(8,128)(2,1)} %copy.45) | copy-start | bytes 3145732
  480.8 383.9 %collective-permute-start = (f32[1024,2048]{1,0:T(8,128)S(1)}, f32[1024,2048]{1,0:T(8,128)}, u32[]{:S(2)}, u32[]{:S(2)}) collective-permute-start(f32[1024,2048]{1,0:T(8,128)S(1)} %convolution_add_fusion), channel_id=1, source_target_pairs={{0,1},{1,0},{2,3},{3,2},{4,5},{5,4},{6,7},{7,6},{8,9},{9,8},{10,11... | collective-permute-start | bytes 25165832 | tf_op jit(solution)/shard_map/ppermute | solution.py:130
  876.5 363.2 %collective-permute-start.1 = (f32[1024,2048]{1,0:T(8,128)}, f32[1024,2048]{1,0:T(8,128)}, u32[]{:S(2)}, u32[]{:S(2)}) collective-permute-start(f32[1024,2048]{1,0:T(8,128)} %add.145), channel_id=1, source_target_pairs={{0,2},{1,3},{2,0},{3,1},{4,6},{5,7},{6,4},{7,5},{8,10},{9,11},{10,... | collective-permute-start | bytes 25165832 | tf_op jit(solution)/shard_map/ppermute | solution.py:130
  (8 other events, 23.0 us)
Sparse Core Ops, SparseCore 0:
  405.1 458.0 all-reduce.2
Sparse Core Ops, SparseCore 1:
  426.0 148.9 reduce-scatter.8
  578.8 50.9 reduce-scatter.6
  633.6 86.7 reduce-scatter.10
  724.4 91.9 reduce-scatter.4
